TPU v7x, 32 devices: a whole 2x2x4 slice. The times are simulated.
32 devices in a mesh: row: 4 (over y, x), col: 8 (over z, core).
Axes of the slice: x: 2, y: 2, z: 4, core: 2. Of those that a mesh axis runs over, the one named last changes fastest.
Arguments:
- teacher: bfloat16 [16384, 256], replicated, may hold values from -4 to 4
- panel_ids: int32 [2048], P('col'), may hold values from 0 to 16383
- rest_ids: int32 [4, 8, 128], P('row', 'col'), may hold values from 0 to 16383
- inverse: bfloat16 [2048, 2048], replicated, may hold values from -1 to 1, as said below
Outputs:
- trailing: float32 [8, 4, 128, 4, 8, 128], P(None, 'row', None, None, 'col')
- panel_rows: bfloat16 [4, 8, 128, 2048], P('row', 'col')
Inputs may be any that keep to these rules, and one draw needn't show every extreme that they name: `inverse`: zero above the diagonal.
All inputs are finite; a program needn't handle non-finite values.
Results may differ from a plain program's by a relative error of at most 0.0049.
Values may be sent and summed in bfloat16 or wider, within the bound.
A program may use at most 128 MiB of HBM per device.

v0:
```python
import jax
import jax.numpy as jnp
from jax import lax
from jax.sharding import PartitionSpec as P


def gaussian(left_rows, right_rows, inv_scale):
    sq_left = jnp.sum(jnp.square(left_rows.astype(jnp.float32)), axis=-1)
    sq_right = jnp.sum(jnp.square(right_rows.astype(jnp.float32)), axis=-1)
    inner = lax.dot_general(
        left_rows, right_rows, (((1,), (1,)), ((), ())), preferred_element_type=jnp.float32
    )
    return jnp.exp(-inv_scale * (sq_left[:, None] + sq_right[None, :] - 2.0 * inner))


def factor(rows_emb, panel_emb, inverse, inv_scale):
    kernel = gaussian(rows_emb, panel_emb, inv_scale).astype(jnp.bfloat16)
    block_width = inverse.shape[0] // 4
    pieces = []
    for block_at in range(4):
        finish = (block_at + 1) * block_width
        pieces.append(
            lax.dot_general(
                kernel[:, :finish],
                inverse[block_at * block_width : finish, :finish],
                (((1,), (1,)), ((), ())),
                preferred_element_type=jnp.float32,
            )
        )
    return jnp.concatenate(pieces, 1).astype(jnp.bfloat16)


def shards(teacher, panel_ids, rest_ids, inverse):
    n_row = lax.axis_size("row")
    n_col = lax.axis_size("col")
    row_at = lax.axis_index("row")
    col_at = lax.axis_index("col")
    stretch_rows = rest_ids.shape[2]
    inv_scale = 2.0 / teacher.shape[1]
    gathered = lax.all_gather(rest_ids, ("row", "col"), axis=0, tiled=True)
    blocks = gathered.reshape(n_row * n_col, stretch_rows)
    panel = lax.all_gather(panel_ids, "col", axis=0, tiled=True)
    panel_emb = teacher[panel]
    own_ids = lax.dynamic_slice_in_dim(blocks, row_at * n_col + col_at, 1, 0).reshape(stretch_rows)
    col_ids = lax.dynamic_slice_in_dim(
        blocks.reshape(n_row, n_col, stretch_rows), col_at, 1, 1
    ).reshape(-1)
    row_ids = lax.dynamic_slice_in_dim(
        blocks.reshape(n_col, n_row, stretch_rows), row_at, 1, 1
    ).reshape(-1)
    own_factor = factor(teacher[own_ids], panel_emb, inverse, inv_scale)
    col_emb = teacher[col_ids]
    col_factor = lax.all_gather(own_factor, "row", axis=0, tiled=True)
    row_emb = teacher[row_ids]
    kernel = gaussian(row_emb, col_emb, inv_scale)
    row_factor = factor(row_emb, panel_emb, inverse, inv_scale)
    update = lax.dot_general(
        row_factor, col_factor, (((1,), (1,)), ((), ())), preferred_element_type=jnp.float32
    )
    rows_local = jnp.arange(n_col * stretch_rows, dtype=jnp.int32)
    row_index = (
        rows_local // stretch_rows * n_row + row_at
    ) * stretch_rows + rows_local % stretch_rows
    cols_local = jnp.arange(n_row * stretch_rows, dtype=jnp.int32)
    col_index = (
        cols_local // stretch_rows * n_col + col_at
    ) * stretch_rows + cols_local % stretch_rows
    result = kernel - update
    trailing = jnp.where(row_index[:, None] >= col_index[None, :], result, jnp.zeros_like(result))
    return (
        trailing.reshape(n_col, 1, stretch_rows, n_row, 1, stretch_rows),
        own_factor.reshape(1, 1, stretch_rows, own_factor.shape[1]),
    )


def solution(mesh):
    return jax.shard_map(
        shards,
        mesh=mesh,
        in_specs=(P(), P("col"), P("row", "col", None), P()),
        out_specs=(P(None, "row", None, None, "col", None), P("row", "col", None, None)),
        check_vma=False,
    )
```

profile of v0, /device:TPU:0, one launch (start us, length us, event | category | flops | bytes accessed | tf_op | source)
XLA Modules:
  0.0 132.2 jit_solution(9935352924947401463)
XLA Ops:
  7.2 0.0 all-gather.3.cloned.1.call-start
  7.2 43.5 %all_gather.9 = s32[32,1,128]{2,1,0:T(1,128)S(1)} all-gather(s32[1,1,128]{2,1,0:T(1,128)} %param.6), channel_id=1, replica_groups=mesh['row'=4,'col'=8] {'row','col'}, dimensions={0}, use_global_device_ids=true | all-gather | bytes 16896 | tf_op jit(solution)/shard_map/all_gather | solution.py:40
  50.7 5.2 %gather_fusion.3 = bf16[128,256]{1,0:T(8,128)(2,1)S(1)} fusion(bf16[16384,256]{1,0:T(8,128)(2,1)} %param.4, s32[1024]{0:T(1024)S(1)} %pad_clamp_fusion), kind=kCustom, calls=%fused_computation.3 | custom fusion | bytes 131584 | tf_op jit(solution)/shard_map/gather | solution.py:51
  55.9 0.1 multiply_reduce_fusion.3
  56.0 9.0 %all-gather = s32[8,1,256]{2,1,0:T(1,128)S(1)} all-gather(s32[1,1,256]{2,1,0:T(1,128)} %bitcast.42), channel_id=1, replica_groups=mesh['row'=4,'col'=8] {'col'}, dimensions={0}, use_global_device_ids=true | all-gather | bytes 9216 | tf_op jit(solution)/shard_map/all_gather | solution.py:42
  65.0 11.1 %gather_fusion.2 = bf16[2048,256]{1,0:T(8,128)(2,1)S(1)} fusion(bf16[16384,256]{1,0:T(8,128)(2,1)} %param.4, s32[2048]{0:T(1024)S(1)} %fusion.46), kind=kCustom, calls=%fused_computation.2 | custom fusion | bytes 2105344 | tf_op jit(solution)/shard_map/gather | solution.py:43
  76.1 0.3 multiply_reduce_fusion
  76.5 0.5 fusion.13
  77.0 1.3 %convolution_convert_fusion.1 = bf16[128,512]{1,0:T(8,128)(2,1)S(1)} fusion(bf16[2048,2048]{1,0:T(8,128)(2,1)} %param.7, bf16[128,2048]{1,0:T(8,128)(2,1)S(1)} %fusion.13), kind=kOutput, calls=%fused_computation.36 | convolution fusion | flops 67174400 | bytes 786432 | tf_op jit(solution)/shard_map/dot_general | solution.py:23
  78.4 1.7 %convolution_convert_fusion.2 = bf16[128,512]{1,0:T(8,128)(2,1)S(1)} fusion(bf16[2048,2048]{1,0:T(8,128)(2,1)} %param.7, bf16[128,2048]{1,0:T(8,128)(2,1)S(1)} %fusion.13), kind=kOutput, calls=%fused_computation.37 | convolution fusion | flops 134283264 | bytes 1441792 | tf_op jit(solution)/shard_map/dot_general | solution.py:23
  80.1 2.4 %fusion.32 = bf16[128,512]{1,0:T(8,128)(2,1)S(1)} fusion(bf16[128,2048]{1,0:T(8,128)(2,1)S(1)} %fusion.13, bf16[2048,2048]{1,0:T(8,128)(2,1)} %param.7), kind=kOutput, calls=%fused_computation.35 | convolution fusion | flops 268500992 | bytes 2752512 | tf_op jit(solution)/shard_map/dot_general | solution.py:23
  82.5 2.1 %fusion.35 = bf16[128,512]{1,0:T(8,128)(2,1)S(1)} fusion(bf16[2048,2048]{1,0:T(8,128)(2,1)} %param.7, bf16[128,2048]{1,0:T(8,128)(2,1)S(1)} %fusion.13), kind=kOutput, calls=%fused_computation.38 | convolution fusion | flops 201392128 | bytes 2097152 | tf_op jit(solution)/shard_map/dot_general | solution.py:23
  84.6 0.8 pad_maximum_fusion
  85.4 0.0 all-gather.3.cloned.1.call-update
  85.5 7.9 %gather_fusion = bf16[1024,256]{1,0:T(8,128)(2,1)S(1)} fusion(bf16[16384,256]{1,0:T(8,128)(2,1)} %param.4, s32[1024]{0:T(1024)S(1)} %broadcast_clamp_fusion), kind=kCustom, calls=%fused_computation | custom fusion | bytes 1052672 | tf_op jit(solution)/shard_map/gather | solution.py:54
  93.4 6.0 %gather_fusion.1 = bf16[512,256]{1,0:T(8,128)(2,1)S(1)} fusion(bf16[16384,256]{1,0:T(8,128)(2,1)} %param.4, s32[1024]{0:T(1024)S(1)} %pad_clamp_fusion.1), kind=kCustom, calls=%fused_computation.1 | custom fusion | bytes 526336 | tf_op jit(solution)/shard_map/gather | solution.py:52
  99.5 0.1 multiply_reduce_fusion.2
  99.7 0.2 multiply_reduce_fusion.1
  99.9 0.0 slice-start
  99.9 0.8 pad_maximum_fusion.1
  100.7 0.0 slice-start.1
  100.7 2.6 %exponential_convert_fusion = bf16[1024,2048]{1,0:T(8,128)(2,1)S(1)} fusion(bf16[1024,256]{1,0:T(8,128)(2,1)S(1)} %gather_fusion, bf16[2048,256]{1,0:T(8,128)(2,1)S(1)} %gather_fusion.2, f32[2048]{0:T(1024)S(1)} %multiply_reduce_fusion, f32[1024]{0:T(1024)S(1)} %multiply_reduce_fusion.1), kind=kOutput, calls=%fused_computation.4 | convolution fusion | flops 1084227584 | bytes 5779456 | tf_op jit(solution)/shard_map/dot_general | solution.py:10
  103.3 0.0 slice-done
  103.3 0.4 slice-done.1
  103.7 0.7 convolution_convert_fusion
  104.4 1.3 fusion.20
  105.7 2.8 %fusion.23 = bf16[1024,512]{1,0:T(8,128)(2,1)} fusion(bf16[1024,2048]{1,0:T(8,128)(2,1)S(1)} %exponential_convert_fusion, bf16[2048,2048]{1,0:T(8,128)(2,1)S(1)} %bitcast.44), kind=kOutput, calls=%fused_computation.29 | convolution fusion | flops 1611137024 | bytes 5767168 | tf_op jit(solution)/shard_map/dot_general | solution.py:23
  108.5 3.3 %fusion.26 = bf16[1024,512]{1,0:T(8,128)(2,1)} fusion(bf16[1024,2048]{1,0:T(8,128)(2,1)S(1)} %exponential_convert_fusion, bf16[2048,2048]{1,0:T(8,128)(2,1)S(1)} %bitcast.44), kind=kOutput, calls=%fused_computation.31 | convolution fusion | flops 2148007936 | bytes 7340032 | tf_op jit(solution)/shard_map/dot_general | solution.py:23
  111.9 6.3 %all-gather.3.cloned.1.call-done = bf16[512,2048]{1,0:T(8,128)(2,1)} async-done(((bf16[128,2048]{1,0:T(8,128)(2,1)}), bf16[512,2048]{1,0:T(8,128)(2,1)}) %all-gather.3.cloned.1.call-update) | async-done | bytes 2097168 | tf_op jit(solution)/shard_map/all_gather | solution.py:53
  118.2 4.5 %fusion = f32[1024,512]{1,0:T(8,128)S(1)} fusion(bf16[512,2048]{1,0:T(8,128)(2,1)} %all-gather.3.cloned.1.call-done, bf16[1024,512]{1,0:T(8,128)(2,1)} %fusion.26, bf16[1024,512]{1,0:T(8,128)(2,1)} %fusion.23, bf16[1024,512]{1,0:T(8,128)(2,1)S(1)} %fusion.20, bf16[1024,512]{1,0:T(8,128)(2,1)S(1)} %convolution_convert_fusion), kind=kOutput, calls=%fused_computation.5 | convolution fusion | flops 2164260864 | bytes 8388608 | tf_op jit(solution)/shard_map/dot_general | solution.py:57
  122.8 0.8 subtract_select_fusion
  123.6 1.7 %reshape.218 = f32[8,1,128,4,1,128]{5,3,2,0,4,1:T(4,128)} reshape(f32[1024,512]{1,0:T(8,128)S(1)} %subtract_select_fusion) | data formatting | bytes 4194304 | tf_op jit(solution)/shard_map/reshape | solution.py:71
  (10 shorter events, 0.1 us)
Async XLA Ops:
  7.2 111.1 %all-gather.3.cloned.1.call-start = ((), (), s32[]{:S(2)}) async-start(), calls=%async_computation | async-start | bytes 2621440 | tf_op jit(solution)/shard_map/all_gather | solution.py:53
  99.9 3.4 %slice-start = ((s8[8388608]{0:T(1024)(128)(4,1)}), s8[4194304]{0:T(1024)(128)(4,1)S(1)}, s32[]{:S(2)}) async-start(s8[8388608]{0:T(1024)(128)(4,1)} %bitcast.43), calls=%async_computation.1 | async-start | bytes 8388608
  100.7 3.0 %slice-start.1 = ((s8[8388608]{0:T(1024)(128)(4,1)}), s8[4194304]{0:T(1024)(128)(4,1)S(1)}, s32[]{:S(2)}) async-start(s8[8388608]{0:T(1024)(128)(4,1)} %bitcast.43), calls=%async_computation.2 | async-start | bytes 8388608
Sparse Core Ops, SparseCore 0:
  85.6 32.6 all-gather.2
where the time goes:
time: 133 us; the launch traced here: 132 us
  blocking collectives  52.5 us (39%)
  local copies, waits for them, and re-layouts  32.4 us (24%)
  matrix products  24.1 us (18%)
  between operations  14.2 us (11%)
  waiting for transfers between devices  6.36 us (5%)
  other arithmetic  2.57 us (2%)
    all_gather x1, blocking collectives, shards(): gathered = lax.all_gather(rest_ids, ('row', 'col'), axis=0, tiled=True)  43.5 us
    dot_general x8, matrix products, factor(): lax.dot_general(kernel[:, :finish], inverse[block_at * block_width:finish...  15.7 us
    gather x1, local copies, waits for them, and re-layouts, shards(): panel_emb = teacher[panel]  11.1 us
    all_gather x1, blocking collectives, shards(): panel = lax.all_gather(panel_ids, 'col', axis=0, tiled=True)  8.99 us
    gather x1, local copies, waits for them, and re-layouts, shards(): row_emb = teacher[row_ids]  7.92 us
    all_gather x1, waiting for transfers between devices, shards(): col_factor = lax.all_gather(own_factor, 'row', axis=0, tiled=True)  6.34 us
    gather x1, local copies, waits for them, and re-layouts, shards(): col_emb = teacher[col_ids]  6.02 us
    gather x1, local copies, waits for them, and re-layouts, shards(): own_factor = factor(teacher[own_ids], panel_emb, inverse, inv_scale)  5.22 us
  transfers between devices with their start and end apart: 1, of which 1 were waited for; matrix products, arithmetic and copies ran while one was open for 20% of the time, Pallas kernels for 0%

commit v1 on v0

--- a/solution.py
+++ b/solution.py
@@ -2,6 +2,29 @@
 import jax.numpy as jnp
 from jax import lax
 from jax.sharding import PartitionSpec as P
+
+
+def face_write(my_tile, along_dim):
+    my_tile = jnp.moveaxis(my_tile, 0, along_dim)
+    w_next = my_tile.shape
+    current_block = my_tile.reshape(
+        *w_next[:along_dim], w_next[along_dim] * w_next[along_dim + 1], *w_next[along_dim + 2 :]
+    )
+    return current_block
+
+
+def perform_heads(local_block, device_axis, d_out):
+    degree = jax.lax.psum(1, device_axis)
+    bank = [(ix, (ix + 1) % degree) for ix in range(degree)]
+    found = [local_block]
+    while len(found) < degree:
+        r_now = jax.lax.ppermute(found[-1], device_axis, bank)
+        found.append(r_now)
+    kept_arr = jax.lax.axis_index(device_axis)
+    f_next = jnp.stack(found, axis=0)
+    found = f_next[(kept_arr - jnp.arange(degree)) % degree]
+    z2 = face_write(found, d_out)
+    return z2
 
 
 def gaussian(left_rows, right_rows, inv_scale):
@@ -39,7 +62,7 @@
     inv_scale = 2.0 / teacher.shape[1]
     gathered = lax.all_gather(rest_ids, ("row", "col"), axis=0, tiled=True)
     blocks = gathered.reshape(n_row * n_col, stretch_rows)
-    panel = lax.all_gather(panel_ids, "col", axis=0, tiled=True)
+    panel = perform_heads(panel_ids, "col", 0)
     panel_emb = teacher[panel]
     own_ids = lax.dynamic_slice_in_dim(blocks, row_at * n_col + col_at, 1, 0).reshape(stretch_rows)
     col_ids = lax.dynamic_slice_in_dim(

time: 133 us -> 153 us (1.15)
  waiting for transfers between devices: 6.36 us -> 34.8 us
  blocking collectives: 52.5 us -> 43 us
    ppermute x0 -> x7, waiting for transfers between devices: none -> 18.7 us  [perform_heads(): r_now = jax.lax.ppermute(found[-1], device_axis, bank)]
    all_gather x1, waiting for transfers between devices: 6.34 us -> 16.1 us  [shards(): col_factor = lax.all_gather(own_factor, 'row', axis=0, tiled=True)]
    all_gather x1 -> x0, blocking collectives: 8.99 us -> none  [shards(): panel = lax.all_gather(panel_ids, 'col', axis=0, tiled=True)]
  transfers between devices with their start and end apart: 1 -> 8, of which waited for: 1 -> 5; matrix products, arithmetic and copies ran while one was open for 20% -> 20% of each run, Pallas kernels for 0% -> 0%
where the time goes in v1:
time: 153 us
  blocking collectives  43 us (28%)
  waiting for transfers between devices  34.8 us (23%)
  local copies, waits for them, and re-layouts  33.2 us (22%)
  matrix products  24.1 us (16%)
  between operations  14.3 us (9%)
  other arithmetic  2.59 us (2%)
    all_gather x1, blocking collectives, shards(): gathered = lax.all_gather(rest_ids, ('row', 'col'), axis=0, tiled=True)  43 us
    ppermute x7, waiting for transfers between devices, perform_heads(): r_now = jax.lax.ppermute(found[-1], device_axis, bank)  18.7 us
    all_gather x1, waiting for transfers between devices, shards(): col_factor = lax.all_gather(own_factor, 'row', axis=0, tiled=True)  16.1 us
    dot_general x8, matrix products, factor(): lax.dot_general(kernel[:, :finish], inverse[block_at * block_width:finish...  15.7 us
    gather x1, local copies, waits for them, and re-layouts, shards(): panel_emb = teacher[panel]  11.1 us
    gather x1, local copies, waits for them, and re-layouts, shards(): row_emb = teacher[row_ids]  7.92 us
    gather x1, local copies, waits for them, and re-layouts, shards(): col_emb = teacher[col_ids]  6.02 us
    gather x1, local copies, waits for them, and re-layouts, shards(): own_factor = factor(teacher[own_ids], panel_emb, inverse, inv_scale)  5.22 us
  transfers between devices with their start and end apart: 8, of which 5 were waited for; matrix products, arithmetic and copies ran while one was open for 20% of the time, Pallas kernels for 0%

profile of v1, /device:TPU:0, one launch (start us, length us, event | category | flops | bytes accessed | tf_op | source)
XLA Modules:
  0.0 153.0 jit_solution(10835155268741538277)
XLA Ops:
  7.2 0.0 copy-start
  7.2 0.0 all-gather.2.cloned.1.call-start
  7.2 0.5 collective-permute-start
  7.8 43.0 %all_gather.6 = s32[32,1,128]{2,1,0:T(1,128)S(1)} all-gather(s32[1,1,128]{2,1,0:T(1,128)} %param.6), channel_id=1, replica_groups=mesh['row'=4,'col'=8] {'row','col'}, dimensions={0}, use_global_device_ids=true | all-gather | bytes 16896 | tf_op jit(solution)/shard_map/all_gather | solution.py:63
  50.8 0.0 collective-permute-done
  50.8 0.4 collective-permute-start.1
  51.2 4.5 %collective-permute-done.1 = s32[256]{0:T(256)S(1)} collective-permute-done((s32[256]{0:T(256)S(1)}, s32[256]{0:T(256)S(1)}, u32[]{:S(2)}, u32[]{:S(2)}) %collective-permute-start.1) | collective-permute-done | bytes 1056 | tf_op jit(solution)/shard_map/ppermute | solution.py:21
  55.7 0.0 collective-permute-start.2
  55.7 5.2 %gather_fusion.4 = bf16[128,256]{1,0:T(8,128)(2,1)S(1)} fusion(bf16[16384,256]{1,0:T(8,128)(2,1)} %param.4, s32[1024]{0:T(1024)S(1)} %pad_clamp_fusion), kind=kCustom, calls=%fused_computation.4 | custom fusion | bytes 131584 | tf_op jit(solution)/shard_map/gather | solution.py:74
  60.9 0.0 collective-permute-done.2
  60.9 0.1 collective-permute-start.3
  61.0 0.1 multiply_reduce_fusion.3
  61.1 4.7 %collective-permute-done.3 = s32[256]{0:T(256)S(1)} collective-permute-done((s32[256]{0:T(256)S(1)}, s32[256]{0:T(256)S(1)}, u32[]{:S(2)}, u32[]{:S(2)}) %collective-permute-start.3) | collective-permute-done | bytes 1056 | tf_op jit(solution)/shard_map/ppermute | solution.py:21
  65.8 0.0 collective-permute-start.4
  65.8 4.8 %collective-permute-done.4 = s32[256]{0:T(256)S(1)} collective-permute-done((s32[256]{0:T(256)S(1)}, s32[256]{0:T(256)S(1)}, u32[]{:S(2)}, u32[]{:S(2)}) %collective-permute-start.4) | collective-permute-done | bytes 1056 | tf_op jit(solution)/shard_map/ppermute | solution.py:21
  70.6 0.0 collective-permute-start.5
  70.6 4.8 %collective-permute-done.5 = s32[256]{0:T(256)S(1)} collective-permute-done((s32[256]{0:T(256)S(1)}, s32[256]{0:T(256)S(1)}, u32[]{:S(2)}, u32[]{:S(2)}) %collective-permute-start.5) | collective-permute-done | bytes 1056 | tf_op jit(solution)/shard_map/ppermute | solution.py:21
  75.4 0.0 collective-permute-start.6
  75.4 7.9 %gather_fusion = bf16[1024,256]{1,0:T(8,128)(2,1)S(1)} fusion(bf16[16384,256]{1,0:T(8,128)(2,1)} %param.4, s32[1024]{0:T(1024)S(1)} %broadcast_clamp_fusion.1), kind=kCustom, calls=%fused_computation | custom fusion | bytes 1052672 | tf_op jit(solution)/shard_map/gather | solution.py:77
  83.3 0.0 collective-permute-done.6
  83.3 0.0 copy-done
  83.4 0.6 gather_fusion.2
  84.0 11.1 %gather_fusion.3 = bf16[2048,256]{1,0:T(8,128)(2,1)S(1)} fusion(bf16[16384,256]{1,0:T(8,128)(2,1)} %param.4, s32[2048]{0:T(1024)S(1)} %broadcast_clamp_fusion), kind=kCustom, calls=%fused_computation.3 | custom fusion | bytes 2105344 | tf_op jit(solution)/shard_map/gather | solution.py:66
  95.1 0.3 multiply_reduce_fusion
  95.4 0.5 fusion.13
  95.9 1.3 convolution_convert_fusion.1
  97.3 1.7 %convolution_convert_fusion.2 = bf16[128,512]{1,0:T(8,128)(2,1)S(1)} fusion(bf16[2048,2048]{1,0:T(8,128)(2,1)} %param.7, bf16[128,2048]{1,0:T(8,128)(2,1)S(1)} %fusion.13), kind=kOutput, calls=%fused_computation.38 | convolution fusion | flops 134283264 | bytes 1441792 | tf_op jit(solution)/shard_map/dot_general | solution.py:46
  99.0 2.4 %fusion.32 = bf16[128,512]{1,0:T(8,128)(2,1)S(1)} fusion(bf16[128,2048]{1,0:T(8,128)(2,1)S(1)} %fusion.13, bf16[2048,2048]{1,0:T(8,128)(2,1)} %param.7), kind=kOutput, calls=%fused_computation.36 | convolution fusion | flops 268500992 | bytes 2752512 | tf_op jit(solution)/shard_map/dot_general | solution.py:46
  101.4 2.1 %fusion.35 = bf16[128,512]{1,0:T(8,128)(2,1)S(1)} fusion(bf16[2048,2048]{1,0:T(8,128)(2,1)} %param.7, bf16[128,2048]{1,0:T(8,128)(2,1)S(1)} %fusion.13), kind=kOutput, calls=%fused_computation.39 | convolution fusion | flops 201392128 | bytes 2097152 | tf_op jit(solution)/shard_map/dot_general | solution.py:46
  103.5 0.8 pad_maximum_fusion
  104.4 0.0 all-gather.2.cloned.1.call-update
  104.4 6.0 %gather_fusion.1 = bf16[512,256]{1,0:T(8,128)(2,1)S(1)} fusion(bf16[16384,256]{1,0:T(8,128)(2,1)} %param.4, s32[1024]{0:T(1024)S(1)} %pad_clamp_fusion.2), kind=kCustom, calls=%fused_computation.1 | custom fusion | bytes 526336 | tf_op jit(solution)/shard_map/gather | solution.py:75
  110.4 0.1 multiply_reduce_fusion.2
  110.6 0.2 multiply_reduce_fusion.1
  110.8 0.0 slice-start
  110.8 0.8 pad_maximum_fusion.1
  111.7 0.0 slice-start.1
  111.7 2.6 %exponential_convert_fusion = bf16[1024,2048]{1,0:T(8,128)(2,1)S(1)} fusion(bf16[1024,256]{1,0:T(8,128)(2,1)S(1)} %gather_fusion, bf16[2048,256]{1,0:T(8,128)(2,1)S(1)} %gather_fusion.3, f32[2048]{0:T(1024)S(1)} %multiply_reduce_fusion, f32[1024]{0:T(1024)S(1)} %multiply_reduce_fusion.1), kind=kOutput, calls=%fused_computation.5 | convolution fusion | flops 1084227584 | bytes 5779456 | tf_op jit(solution)/shard_map/dot_general | solution.py:33
  114.2 0.0 slice-done
  114.3 0.6 slice-done.1
  114.8 0.7 convolution_convert_fusion
  115.6 1.3 fusion.20
  116.8 2.8 %fusion.23 = bf16[1024,512]{1,0:T(8,128)(2,1)} fusion(bf16[1024,2048]{1,0:T(8,128)(2,1)S(1)} %exponential_convert_fusion, bf16[2048,2048]{1,0:T(8,128)(2,1)S(1)} %bitcast.66), kind=kOutput, calls=%fused_computation.30 | convolution fusion | flops 1611137024 | bytes 5767168 | tf_op jit(solution)/shard_map/dot_general | solution.py:46
  119.7 3.3 %fusion.26 = bf16[1024,512]{1,0:T(8,128)(2,1)} fusion(bf16[1024,2048]{1,0:T(8,128)(2,1)S(1)} %exponential_convert_fusion, bf16[2048,2048]{1,0:T(8,128)(2,1)S(1)} %bitcast.66), kind=kOutput, calls=%fused_computation.32 | convolution fusion | flops 2148007936 | bytes 7340032 | tf_op jit(solution)/shard_map/dot_general | solution.py:46
  123.0 16.1 %all-gather.2.cloned.1.call-done = bf16[512,2048]{1,0:T(8,128)(2,1)} async-done(((bf16[128,2048]{1,0:T(8,128)(2,1)}), bf16[512,2048]{1,0:T(8,128)(2,1)}) %all-gather.2.cloned.1.call-update) | async-done | bytes 2097168 | tf_op jit(solution)/shard_map/all_gather | solution.py:76
  139.0 4.5 %fusion = f32[1024,512]{1,0:T(8,128)S(1)} fusion(bf16[512,2048]{1,0:T(8,128)(2,1)} %all-gather.2.cloned.1.call-done, bf16[1024,512]{1,0:T(8,128)(2,1)} %fusion.26, bf16[1024,512]{1,0:T(8,128)(2,1)} %fusion.23, bf16[1024,512]{1,0:T(8,128)(2,1)S(1)} %fusion.20, bf16[1024,512]{1,0:T(8,128)(2,1)S(1)} %convolution_convert_fusion), kind=kOutput, calls=%fused_computation.6 | convolution fusion | flops 2164260864 | bytes 8388608 | tf_op jit(solution)/shard_map/dot_general | solution.py:80
  143.6 0.8 subtract_select_fusion
  144.4 1.7 %reshape.299 = f32[8,1,128,4,1,128]{5,3,2,0,4,1:T(4,128)} reshape(f32[1024,512]{1,0:T(8,128)S(1)} %subtract_select_fusion) | data formatting | bytes 4194304 | tf_op jit(solution)/shard_map/reshape | solution.py:94
  (15 shorter events, 0.1 us)
Async XLA Ops:
  7.2 76.2 %copy-start = (s32[256]{0:T(256)S(1)}, s32[256]{0:T(256)}, u32[]{:S(2)}) copy-start(s32[256]{0:T(256)} %param.5) | copy-start | bytes 3076
  7.2 131.9 %all-gather.2.cloned.1.call-start = ((), (), s32[]{:S(2)}) async-start(), calls=%async_computation | async-start | bytes 2621440 | tf_op jit(solution)/shard_map/all_gather | solution.py:76
  7.2 43.6 %collective-permute-start = (s32[256]{0:T(256)}, s32[256]{0:T(256)S(1)}, u32[]{:S(2)}, u32[]{:S(2)}) collective-permute-start(s32[256]{0:T(256)} %param.5), channel_id=1, source_target_pairs={{0,1},{1,2},{2,3},{3,4},{4,5},{5,6},{6,7},{7,0},{8,9},{9,10},{10,1... | collective-permute-start | bytes 3080 | tf_op jit(solution)/shard_map/ppermute | solution.py:21
  50.8 4.8 %collective-permute-start.1 = (s32[256]{0:T(256)S(1)}, s32[256]{0:T(256)S(1)}, u32[]{:S(2)}, u32[]{:S(2)}) collective-permute-start(s32[256]{0:T(256)S(1)} %collective-permute-done), channel_id=1, source_target_pairs={{0,1},{1,2},{2,3},{3,4},{4,5},{5,6},{6,7},{7,0},{8,9},{9,10},{10,1... | collective-permute-start | bytes 3080 | tf_op jit(solution)/shard_map/ppermute | solution.py:21
  55.7 5.2 %collective-permute-start.2 = (s32[256]{0:T(256)S(1)}, s32[256]{0:T(256)S(1)}, u32[]{:S(2)}, u32[]{:S(2)}) collective-permute-start(s32[256]{0:T(256)S(1)} %collective-permute-done.1), channel_id=1, source_target_pairs={{0,1},{1,2},{2,3},{3,4},{4,5},{5,6},{6,7},{7,0},{8,9},{9,10},{10,1... | collective-permute-start | bytes 3080 | tf_op jit(solution)/shard_map/ppermute | solution.py:21
  60.9 4.8 %collective-permute-start.3 = (s32[256]{0:T(256)S(1)}, s32[256]{0:T(256)S(1)}, u32[]{:S(2)}, u32[]{:S(2)}) collective-permute-start(s32[256]{0:T(256)S(1)} %collective-permute-done.2), channel_id=1, source_target_pairs={{0,1},{1,2},{2,3},{3,4},{4,5},{5,6},{6,7},{7,0},{8,9},{9,10},{10,1... | collective-permute-start | bytes 3080 | tf_op jit(solution)/shard_map/ppermute | solution.py:21
  65.8 4.8 %collective-permute-start.4 = (s32[256]{0:T(256)S(1)}, s32[256]{0:T(256)S(1)}, u32[]{:S(2)}, u32[]{:S(2)}) collective-permute-start(s32[256]{0:T(256)S(1)} %collective-permute-done.3), channel_id=1, source_target_pairs={{0,1},{1,2},{2,3},{3,4},{4,5},{5,6},{6,7},{7,0},{8,9},{9,10},{10,1... | collective-permute-start | bytes 3080 | tf_op jit(solution)/shard_map/ppermute | solution.py:21
  70.6 4.8 %collective-permute-start.5 = (s32[256]{0:T(256)S(1)}, s32[256]{0:T(256)S(1)}, u32[]{:S(2)}, u32[]{:S(2)}) collective-permute-start(s32[256]{0:T(256)S(1)} %collective-permute-done.4), channel_id=1, source_target_pairs={{0,1},{1,2},{2,3},{3,4},{4,5},{5,6},{6,7},{7,0},{8,9},{9,10},{10,1... | collective-permute-start | bytes 3080 | tf_op jit(solution)/shard_map/ppermute | solution.py:21
  75.4 7.9 %collective-permute-start.6 = (s32[256]{0:T(256)S(1)}, s32[256]{0:T(256)S(1)}, u32[]{:S(2)}, u32[]{:S(2)}) collective-permute-start(s32[256]{0:T(256)S(1)} %collective-permute-done.5), channel_id=1, source_target_pairs={{0,1},{1,2},{2,3},{3,4},{4,5},{5,6},{6,7},{7,0},{8,9},{9,10},{10,1... | collective-permute-start | bytes 3080 | tf_op jit(solution)/shard_map/ppermute | solution.py:21
  110.8 3.4 %slice-start = ((s8[8388608]{0:T(1024)(128)(4,1)}), s8[4194304]{0:T(1024)(128)(4,1)S(1)}, s32[]{:S(2)}) async-start(s8[8388608]{0:T(1024)(128)(4,1)} %bitcast.65), calls=%async_computation.1 | async-start | bytes 8388608
  111.7 3.1 %slice-start.1 = ((s8[8388608]{0:T(1024)(128)(4,1)}), s8[4194304]{0:T(1024)(128)(4,1)S(1)}, s32[]{:S(2)}) async-start(s8[8388608]{0:T(1024)(128)(4,1)} %bitcast.65), calls=%async_computation.2 | async-start | bytes 8388608
Sparse Core Ops, SparseCore 0:
  104.5 34.5 all-gather.1
